TPU v7x, 512 devices: a whole 4x8x8 slice. The times are simulated.
512 devices in a mesh: rep: 16 (over y, core), tp: 32 (over z, x).
Axes of the slice: x: 4, y: 8, z: 8, core: 2. Of those that a mesh axis runs over, the one named last changes fastest.
Arguments:
- tokens: bfloat16 [8192, 8192], P('rep', 'tp'), may hold values from -6 to 6
- base_weight: bfloat16 [8192, 8192], P(None, 'tp'), may hold values from -0.0625 to 0.0625
- delta: bfloat16 [48, 64, 2, 128, 128], P('rep', 'tp'), may hold values from -0.375 to 0.375
- live_blocks: int32 [48, 64, 2], P(None, 'tp'), may hold values from 0 to 63, as said below
- row_variant: int32 [8192, 1], P('rep'), may hold values from 0 to 47; in each aligned block of 512 rows (0 to 511, 512 to 1023, ...) at most 21 rows name the same one
Outputs:
- projected: bfloat16 [8192, 8192], P('rep', 'tp')
Inputs may be any that keep to these rules, and one draw needn't show every extreme that they name: `live_blocks`: the 2 block rows listed for one variant and column block are distinct. `row_variant`: among the rows of one index of rep no variant appears more than 21 times, and some variant appears exactly 21 times.
All inputs are finite; a program needn't handle non-finite values.
Results may differ from a plain program's by a relative error of at most 0.0039.
Values may be sent and summed in bfloat16 or wider, within the bound.
A program may use at most 128 MiB of HBM per device.

v0:
```python
import jax
import jax.numpy as jnp
from jax import lax
from jax.sharding import PartitionSpec as P


def multiply(received, weight_tables):
    sources, local_variants, slot_count, feat_width = received.shape
    col_blocks = weight_tables.shape[1]
    block_size = weight_tables.shape[3]
    shaped = received.reshape(
        sources, local_variants, slot_count, col_blocks, feat_width // col_blocks
    )
    flat_weights = weight_tables.reshape(
        local_variants, col_blocks, feat_width // col_blocks, block_size
    )
    result = jnp.einsum(
        "auncf,ucfb->auncb", shaped, flat_weights, preferred_element_type=jnp.float32
    )
    return result.astype(jnp.bfloat16).reshape(
        sources, local_variants, slot_count, col_blocks * block_size
    )


def local(tokens, base_weight, delta, live_blocks, row_variant):
    rep_count = lax.axis_size("rep")
    local_variants = delta.shape[0]
    col_blocks = delta.shape[1]
    live_count = delta.shape[2]
    block_size = delta.shape[3]
    variants = local_variants * rep_count
    row_count = tokens.shape[0]
    capacity = max(2, 2 * row_count // variants)
    feat_width = col_blocks * live_count * block_size
    features_all = lax.all_gather(tokens, "tp", axis=1, tiled=True)
    base_part = jnp.dot(features_all, base_weight, preferred_element_type=jnp.float32)
    variant = row_variant[:, 0]
    onehot = (variant[:, None] == jnp.arange(variants, dtype=jnp.int32)[None, :]).astype(jnp.int32)
    row_rank = jnp.sum((jnp.cumsum(onehot, axis=0) - 1) * onehot, axis=1)
    slot_index = variant * capacity + row_rank
    tile_indices = jnp.take(live_blocks, variant, axis=0).reshape(
        row_count, col_blocks * live_count
    )
    blocks_view = features_all.reshape(row_count, features_all.shape[1] // block_size, block_size)
    picked = jnp.take_along_axis(blocks_view, tile_indices[:, :, None], axis=1).reshape(
        row_count, feat_width
    )
    outgoing = jnp.zeros((variants * capacity, feat_width), jnp.bfloat16).at[slot_index].set(picked)
    all_deltas = lax.all_gather(delta, "rep", axis=0, tiled=True)
    returned = multiply(outgoing.reshape(1, variants, capacity, feat_width), all_deltas)
    returned_flat = returned.reshape(variants * capacity, col_blocks * block_size)
    correction_summand = jnp.take(returned_flat, slot_index, axis=0)
    return (base_part + correction_summand.astype(jnp.float32)).astype(jnp.bfloat16)


def solution(mesh):
    placed = (
        P("rep", "tp"),
        P(None, "tp"),
        P("rep", "tp", None, None, None),
        P(None, "tp", None),
        P("rep", None),
    )
    return jax.shard_map(
        local, mesh=mesh, in_specs=placed, out_specs=P("rep", "tp"), check_vma=False
    )
```

profile of v0, /device:TPU:1, one launch (start us, length us, event | category | flops | bytes accessed | tf_op | source)
XLA Modules:
  0.0 194.5 jit_solution(5336732794186079991)
XLA Ops:
  6.5 0.0 all-gather.3.cloned.1.call-start
  6.5 0.7 all-gather.3.cloned.1.call-update
  7.3 0.0 all-gather.5.cloned.1.call-start
  7.3 0.7 all-gather.5.cloned.1.call-update
  8.0 0.7 fusion.9
  8.7 1.2 reduce-window.6
  9.9 0.2 slice_reduce_fusion
  10.2 0.8 copy.20
  11.0 0.8 fusion.8
  11.7 0.7 and_reduce_fusion
  12.5 2.1 %gather_fusion = s32[512,2,2]{2,1,0:T(2,128)S(1)} fusion(s32[48,2,2]{2,1,0:T(2,128)S(1)} %copy.20, s32[1024]{0:T(1024)S(1)} %pad_clamp_fusion.1), kind=kCustom, calls=%fused_computation | custom fusion | bytes 18432 | tf_op jit(solution)/shard_map/jit(_take)/gather | solution.py:41
  14.6 0.2 copy.21
  14.8 0.1 copy.24
  15.0 0.2 reshape.171
  15.2 0.2 copy.22
  15.4 105.8 %all-gather.3.cloned.1.call-done = bf16[512,8192]{1,0:T(8,128)(2,1)} async-done(((bf16[512,256]{1,0:T(8,128)(2,1)}), bf16[512,8192]{1,0:T(8,128)(2,1)}) %all-gather.3.cloned.1.call-update) | async-done | bytes 8388624 | tf_op jit(solution)/shard_map/all_gather | solution.py:35
  121.1 9.3 %copy.28 = bf16[64,8,64,128]{3,2,1,0:T(8,128)(2,1)} copy(bf16[64,8,64,128]{3,1,2,0:T(8,128)(2,1)} %bitcast.50) | data formatting | bytes 16777216
  130.4 24.3 %gather_fusion.2 = bf16[2048,128]{1,0:T(8,128)(2,1)S(1)} fusion(bf16[512,64,128]{2,1,0:T(8,128)(2,1)} %bitcast.48, s32[2048]{0:T(1024)S(1)} %reshape.171), kind=kCustom, calls=%fused_computation.2 | custom fusion | bytes 1064960 | tf_op jit(solution)/shard_map/jit(take_along_axis)/gather | solution.py:45
  154.8 1.6 broadcast_select_fusion
  156.4 2.7 %scatter_custom_fusion = bf16[1008,512]{1,0:T(8,128)(2,1)S(1)} fusion(s32[512]{0:T(512)S(1)} %bitcast.58, bf16[64,8,4,128]{3,2,1,0:T(4,128)(2,1)S(1)} %bitcast.52, bf16[]{:T(256)} %constant.50.clone.1), kind=kCustom, calls=%fused_computation.9 | custom fusion | bytes 1556482 | tf_op jit(solution)/shard_map/scatter | solution.py:48
  159.1 0.2 reshape.153
  159.4 14.4 %all-gather.5.cloned.1.call-done = bf16[48,2,2,128,128]{4,3,2,1,0:T(8,128)(2,1)} async-done(((bf16[3,2,2,128,128]{4,3,2,1,0:T(8,128)(2,1)}), bf16[48,2,2,128,128]{4,3,2,1,0:T(8,128)(2,1)}) %all-gather.5.cloned.1.call-update) | async-done | bytes 6291472 | tf_op jit(solution)/shard_map/all_gather | solution.py:49
  173.8 3.8 %fusion = bf16[1,48,21,2,128]{4,2,3,1,0:T(8,128)(2,1)S(1)} fusion(bf16[48,2,256,128]{3,2,1,0:T(8,128)(2,1)} %bitcast.51, bf16[48,21,2,256]{3,2,1,0:T(2,128)(2,1)S(1)} %reshape.153), kind=kOutput, calls=%fused_computation.5 | convolution fusion | flops 132378624 | bytes 7839744 | tf_op jit(solution)/shard_map/auncf,ucfb->auncb/dot_general | solution.py:17
  177.6 0.4 copy.26
  178.0 0.1 copy.39
  178.1 2.0 %gather_fusion.1 = bf16[512,256]{1,0:T(8,128)(2,1)S(1)} fusion(bf16[1008,256]{1,0:T(8,128)(2,1)S(1)} %bitcast.49, s32[1024]{0:T(1024)S(1)} %pad_clamp_fusion), kind=kCustom, calls=%fused_computation.1 | custom fusion | bytes 526336 | tf_op jit(solution)/shard_map/jit(_take)/gather | solution.py:52
  180.1 7.6 %fusion.1 = bf16[512,256]{1,0:T(8,128)(2,1)} fusion(bf16[512,8192]{1,0:T(8,128)(2,1)} %all-gather.3.cloned.1.call-done, bf16[8192,256]{1,0:T(8,128)(2,1)} %param.6, bf16[512,256]{1,0:T(8,128)(2,1)S(1)} %gather_fusion.1, pred[512]{0:T(512)(128)(4,1)S(1)} %get-tuple-element.9), kind=kOutput, calls=%fused_computation.7 | convolution fusion | flops 2148007936 | bytes 13107712 | tf_op jit(solution)/shard_map/dot_general | solution.py:36
  (8 shorter events, 0.1 us)
Async XLA Ops:
  6.5 114.6 %all-gather.3.cloned.1.call-start = ((), (), s32[]{:S(2)}) async-start(), calls=%async_computation | async-start | bytes 8650752 | tf_op jit(solution)/shard_map/all_gather | solution.py:35
  7.3 166.5 %all-gather.5.cloned.1.call-start = ((), (), s32[]{:S(2)}) async-start(), calls=%async_computation.1 | async-start | bytes 6684672 | tf_op jit(solution)/shard_map/all_gather | solution.py:49
Sparse Core Ops, SparseCore 0:
  10.4 110.7 all-gather.2
  123.3 50.4 all-gather.4
where the time goes:
time: 195 us
  waiting for transfers between devices  122 us (63%)
  local copies, waits for them, and re-layouts  42.9 us (22%)
  between operations  13.5 us (7%)
  matrix products  11.4 us (6%)
  other arithmetic  5.09 us (3%)
    all_gather x1, waiting for transfers between devices, local(): features_all = lax.all_gather(tokens, 'tp', axis=1, tiled=True)  106 us
    gather x3, local copies, waits for them, and re-layouts, local(): jnp.take_along_axis(blocks_view, tile_indices[:, :, None], axis=1)  24.6 us
    all_gather x1, waiting for transfers between devices, local(): all_deltas = lax.all_gather(delta, 'rep', axis=0, tiled=True)  14.4 us
    unnamed x3, local copies, waits for them, and re-layouts  10.2 us
    dot_general x1, matrix products, local(): jnp.dot(features_all, base_weight, preferred_element_type=jnp.float32)  7.61 us
  transfers between devices with their start and end apart: 2, of which 2 were waited for; matrix products, arithmetic and copies ran while one was open for 23% of the time, Pallas kernels for 0%

commit v1 on v0

--- a/solution.py
+++ b/solution.py
@@ -46,7 +46,9 @@
         row_count, feat_width
     )
     outgoing = jnp.zeros((variants * capacity, feat_width), jnp.bfloat16).at[slot_index].set(picked)
-    all_deltas = lax.all_gather(delta, "rep", axis=0, tiled=True)
+    all_deltas = jnp.concatenate(
+        lax.all_to_all(jnp.stack([delta] * lax.axis_size("rep")), "rep", 0, 0), axis=0
+    )
     returned = multiply(outgoing.reshape(1, variants, capacity, feat_width), all_deltas)
     returned_flat = returned.reshape(variants * capacity, col_blocks * block_size)
     correction_summand = jnp.take(returned_flat, slot_index, axis=0)

time: 195 us -> 184 us (0.944)
  waiting for transfers between devices: 122 us -> 96.2 us
  starting transfers between devices: 0.04 us -> 11.3 us
  local copies, waits for them, and re-layouts: 42.9 us -> 47.6 us
  other arithmetic: 5.09 us -> 3.05 us
    all_gather x1 -> x0, waiting for transfers between devices: 14.4 us -> none  [local(): all_deltas = lax.all_gather(delta, 'rep', axis=0, tiled=True)]
    all_gather x1, waiting for transfers between devices: 106 us -> 92.8 us  [local(): features_all = lax.all_gather(tokens, 'tp', axis=1, tiled=True)]
    all_to_all x0 -> x1, starting transfers between devices: none -> 11.3 us  [local(): lax.all_to_all(jnp.stack([delta] * lax.axis_size('rep')), 'rep', 0, 0)]
    another operation x2 -> x3, local copies, waits for them, and re-layouts: 0.24 us -> 5.49 us  [the longest x1 5.24 us: local(): jnp.stack([delta] * lax.axis_size('rep'))]
    all_to_all x0 -> x1, waiting for transfers between devices: none -> 2.7 us  [local(): lax.all_to_all(jnp.stack([delta] * lax.axis_size('rep')), 'rep', 0, 0)]
    unnamed x3 -> x7, local copies, waits for them, and re-layouts: 10.2 us -> 9.5 us
  transfers between devices with their start and end apart: 2 -> 2, of which waited for: 2 -> 2; matrix products, arithmetic and copies ran while one was open for 23% -> 26% of each run, Pallas kernels for 0% -> 0%
where the time goes in v1:
time: 184 us; the launch traced here: 183 us
  waiting for transfers between devices  96.2 us (52%)
  local copies, waits for them, and re-layouts  47.6 us (26%)
  between operations  13.5 us (7%)
  matrix products  11.4 us (6%)
  starting transfers between devices  11.3 us (6%)
  other arithmetic  3.05 us (2%)
    all_gather x1, waiting for transfers between devices, local(): features_all = lax.all_gather(tokens, 'tp', axis=1, tiled=True)  92.8 us
    gather x3, local copies, waits for them, and re-layouts, local(): jnp.take_along_axis(blocks_view, tile_indices[:, :, None], axis=1)  24.6 us
    all_to_all x1, starting transfers between devices, local(): lax.all_to_all(jnp.stack([delta] * lax.axis_size('rep')), 'rep', 0, 0)  11.3 us
    unnamed x7, local copies, waits for them, and re-layouts  9.5 us
    dot_general x1, matrix products, local(): jnp.dot(features_all, base_weight, preferred_element_type=jnp.float32)  7.61 us
    another operation x1, local copies, waits for them, and re-layouts, local(): jnp.stack([delta] * lax.axis_size('rep'))  5.24 us
    dot_general x1, matrix products, multiply(): jnp.einsum('auncf,ucfb->auncb', shaped, flat_weights, preferred_element_t...  3.82 us
  transfers between devices with their start and end apart: 2, of which 2 were waited for; matrix products, arithmetic and copies ran while one was open for 26% of the time, Pallas kernels for 0%

profile of v1, /device:TPU:1, one launch (start us, length us, event | category | flops | bytes accessed | tf_op | source)
XLA Modules:
  0.0 183.1 jit_solution(10730475682341761476)
XLA Ops:
  6.5 0.0 all-gather.2.cloned.1.call-start
  6.5 0.7 all-gather.2.cloned.1.call-update
  7.3 5.2 %stack.2 = bf16[16,3,2,2,128,128]{5,4,3,2,1,0:T(8,128)(2,1)} broadcast(bf16[3,2,2,128,128]{4,3,2,1,0:T(8,128)(2,1)} %param.7), dimensions={1,2,3,4,5} | broadcast | bytes 6684672 | tf_op jit(solution)/shard_map/stack | solution.py:50
  12.5 0.0 copy-start
  12.5 0.0 copy-start.1
  12.5 11.3 %all-to-all-start = ((bf16[16,3,2,2,128,128]{5,4,3,2,1,0:T(8,128)(2,1)}), bf16[16,3,2,2,128,128]{5,4,3,2,1,0:T(8,128)(2,1)}, u32[]{:S(2)}, u32[]{:S(2)}) async-start(bf16[16,3,2,2,128,128]{5,4,3,2,1,0:T(8,128)(2,1)} %stack.2), calls=%async_computation | async-start | bytes 12582912 | tf_op jit(solution)/shard_map/all_to_all | solution.py:50
  23.8 0.0 copy-done
  23.9 1.2 reduce-window.6
  25.1 0.2 slice_reduce_fusion
  25.3 0.0 copy-done.1
  25.3 0.1 copy.12
  25.4 0.1 fusion.8
  25.6 2.1 %gather_fusion = s32[512,2,2]{2,1,0:T(2,128)S(1)} fusion(s32[48,2,2]{2,1,0:T(2,128)S(1)} %copy.12, s32[1024]{0:T(1024)S(1)} %pad_clamp_fusion.1), kind=kCustom, calls=%fused_computation | custom fusion | bytes 18432 | tf_op jit(solution)/shard_map/jit(_take)/gather | solution.py:41
  27.7 0.2 copy.13
  27.9 0.1 copy.16
  28.1 0.2 reshape.169
  28.3 0.2 copy.14
  28.5 92.8 %all-gather.2.cloned.1.call-done = bf16[512,8192]{1,0:T(8,128)(2,1)} async-done(((bf16[512,256]{1,0:T(8,128)(2,1)}), bf16[512,8192]{1,0:T(8,128)(2,1)}) %all-gather.2.cloned.1.call-update) | async-done | bytes 8388624 | tf_op jit(solution)/shard_map/all_gather | solution.py:35
  121.3 9.3 %copy.20 = bf16[64,8,64,128]{3,2,1,0:T(8,128)(2,1)} copy(bf16[64,8,64,128]{3,1,2,0:T(8,128)(2,1)} %bitcast.50) | data formatting | bytes 16777216
  130.6 24.3 %gather_fusion.2 = bf16[2048,128]{1,0:T(8,128)(2,1)S(1)} fusion(bf16[512,64,128]{2,1,0:T(8,128)(2,1)} %bitcast.48, s32[2048]{0:T(1024)S(1)} %reshape.169), kind=kCustom, calls=%fused_computation.2 | custom fusion | bytes 1064960 | tf_op jit(solution)/shard_map/jit(take_along_axis)/gather | solution.py:45
  154.9 1.6 broadcast_select_fusion
  156.6 2.9 %scatter_custom_fusion = bf16[1008,512]{1,0:T(8,128)(2,1)S(1)} fusion(s32[512]{0:T(512)S(1)} %bitcast.57, bf16[64,8,4,128]{3,2,1,0:T(4,128)(2,1)S(1)} %bitcast.51, bf16[]{:T(256)} %constant.50.clone.1), kind=kCustom, calls=%fused_computation.9 | custom fusion | bytes 1556482 | tf_op jit(solution)/shard_map/scatter | solution.py:48
  159.4 0.2 reshape.152
  159.7 2.7 %all-to-all-done = bf16[16,3,2,2,128,128]{5,4,3,2,1,0:T(8,128)(2,1)} async-done(((bf16[16,3,2,2,128,128]{5,4,3,2,1,0:T(8,128)(2,1)}), bf16[16,3,2,2,128,128]{5,4,3,2,1,0:T(8,128)(2,1)}, u32[]{:S(2)}, u32[]{:S(2)}) %all-to-all-start) | async-done | bytes 6291488 | tf_op jit(solution)/shard_map/all_to_all | solution.py:50
  162.4 3.8 %fusion = bf16[1,48,21,2,128]{4,2,3,1,0:T(8,128)(2,1)S(1)} fusion(bf16[48,2,256,128]{3,2,1,0:T(8,128)(2,1)} %bitcast.7, bf16[48,21,2,256]{3,2,1,0:T(2,128)(2,1)S(1)} %reshape.152), kind=kOutput, calls=%fused_computation.5 | convolution fusion | flops 132378624 | bytes 7839744 | tf_op jit(solution)/shard_map/auncf,ucfb->auncb/dot_general | solution.py:17
  166.2 0.4 copy.18
  166.6 0.1 copy.31
  166.7 2.0 %gather_fusion.1 = bf16[512,256]{1,0:T(8,128)(2,1)S(1)} fusion(bf16[1008,256]{1,0:T(8,128)(2,1)S(1)} %bitcast.49, s32[1024]{0:T(1024)S(1)} %pad_clamp_fusion), kind=kCustom, calls=%fused_computation.1 | custom fusion | bytes 526336 | tf_op jit(solution)/shard_map/jit(_take)/gather | solution.py:54
  168.7 7.6 %fusion.1 = bf16[512,256]{1,0:T(8,128)(2,1)} fusion(bf16[512,8192]{1,0:T(8,128)(2,1)} %all-gather.2.cloned.1.call-done, bf16[8192,256]{1,0:T(8,128)(2,1)} %param.6, bf16[512,256]{1,0:T(8,128)(2,1)S(1)} %gather_fusion.1, pred[512]{0:T(512)(128)(4,1)S(1)} %get-tuple-element.9), kind=kOutput, calls=%fused_computation.7 | convolution fusion | flops 2148007936 | bytes 13107712 | tf_op jit(solution)/shard_map/dot_general | solution.py:36
  (10 shorter events, 0.2 us)
Async XLA Ops:
  6.5 114.8 %all-gather.2.cloned.1.call-start = ((), (), s32[]{:S(2)}) async-start(), calls=%async_computation.1 | async-start | bytes 8650752 | tf_op jit(solution)/shard_map/all_gather | solution.py:35
  12.5 11.3 %copy-start = (s32[512,1]{0,1:T(1,128)S(1)}, s32[512,1]{0,1:T(1,128)}, u32[]{:S(2)}) copy-start(s32[512,1]{0,1:T(1,128)} %param.9) | copy-start | bytes 6148
  12.5 12.8 %copy-start.1 = (s32[48,2,2]{0,2,1:T(2,128)S(1)}, s32[48,2,2]{0,2,1:T(2,128)}, u32[]{:S(2)}) copy-start(s32[48,2,2]{0,2,1:T(2,128)} %param.8) | copy-start | bytes 2308
  12.5 149.9 %all-to-all-start = ((bf16[16,3,2,2,128,128]{5,4,3,2,1,0:T(8,128)(2,1)}), bf16[16,3,2,2,128,128]{5,4,3,2,1,0:T(8,128)(2,1)}, u32[]{:S(2)}, u32[]{:S(2)}) async-start(bf16[16,3,2,2,128,128]{5,4,3,2,1,0:T(8,128)(2,1)} %stack.2), calls=%async_computation | async-start | bytes 12582912 | tf_op jit(solution)/shard_map/all_to_all | solution.py:50
Sparse Core Ops, SparseCore 0:
  10.4 110.8 all-gather.1
